TPU v7x, 256 devices: a whole 4x4x8 slice. The times are simulated.
256 devices in a mesh: blk: 256 (over y, z, x, core).
Axes of the slice: x: 4, y: 4, z: 8, core: 2. Of those that a mesh axis runs over, the one named last changes fastest.
Arguments:
- tensor_blocks: bfloat16 [512, 32, 32, 1024], P('blk')
- block_index: int32 [512, 4], P('blk'), may hold values from 0 to 8, as said below
- starts: float32 [256, 256], P(None, 'blk'), may hold values from -6 to 6
- shifts: float32 [256], replicated, may hold values from 0.5 to 2
Outputs:
- iterate: float32 [256, 256], P(None, 'blk')
- estimate: float32 [256], P('blk')
Inputs may be any that keep to these rules, and one draw needn't show every extreme that they name: `block_index`: every sorted quadruple i <= j <= k <= l of 0 to 7 is held by exactly one slot; every other slot holds 8 in all four entries and is not used. A live slot's block is unchanged when two of its axes with equal block indices are swapped.
All inputs are finite; a program needn't handle non-finite values.
Results may differ from a plain program's by a relative error of at most 0.009.
Values sent between devices are 32-bit elements; how exact they have to be, the bound alone decides.
A program may use at most 64 MiB of HBM per device.

v0:
```python
import jax
import jax.numpy as jnp
from jax import lax
from jax.sharding import Mesh
from jax.sharding import PartitionSpec as P

NSIZE = 256
ITERS = 2
BLK = ("blk_0", "blk_1", "blk_2", "blk_3")


letters = "abcd"


def from_everyone(x, axis):
    count = lax.axis_size(axis)
    return lax.all_to_all(jnp.broadcast_to(x[None], (count, *x.shape)), axis, 0, 0, tiled=True)


def laid_out(blocks, dim):
    dims = list(blocks.shape[1:])
    dims[dim] *= blocks.shape[0]
    return jnp.moveaxis(blocks, 0, dim).reshape(dims)


def gather_axes(x, axes, dim):
    far, near = axes
    blocks = from_everyone(from_everyone(x, far), near)
    return laid_out(blocks.swapaxes(0, 1).reshape(-1, *x.shape), dim)


def rows_for(lines, count):
    spare = -lines.shape[0] % count
    if not spare:
        return lines
    return jnp.concatenate([lines, jnp.zeros((spare, *lines.shape[1:]), lines.dtype)])


def cut_along(x, dim, count):
    before, after = (x.shape[:dim], x.shape[dim + 1 :])
    return jnp.moveaxis(x.reshape(*before, count, -1, *after), dim, 0)


def summed_on_arrival(x, axis, dim):
    count = lax.axis_size(axis)
    blocks = lax.all_to_all(cut_along(x, dim, count), axis, 0, 0, tiled=True)
    return jnp.sum(blocks, axis=0)


def summed_rows(x, axes, dim):
    far, near = axes
    blocks = cut_along(x, dim, lax.axis_size(far))
    nearer = summed_on_arrival(blocks, near, dim + 1)
    arrived = lax.all_to_all(nearer, far, split_axis=0, concat_axis=0, tiled=True)
    return arrived.sum(axis=0)


def sum_by_parts(x, axes):
    lines = x.reshape(-1, x.shape[-1])
    padded = rows_for(lines, lax.axis_size(axes[0]) * lax.axis_size(axes[1]))
    whole = gather_axes(summed_rows(padded, axes, 0), axes, 0)
    return lax.slice_in_dim(whole, 0, len(lines)).reshape(x.shape)


def normalize(values):
    return values * lax.rsqrt(jnp.mean(values * values, axis=0) + 1e-06)


def equal_counts(indices, position):
    earlier = jnp.float32(0.0)
    same_count = jnp.float32(0.0)
    for other in range(4):
        match_value = (indices[other] == indices[position]).astype(jnp.float32)
        same_count = same_count + match_value
        if other < position:
            earlier = earlier + match_value
    return (earlier, same_count)


def factor_product(indices):
    product = jnp.float32(1.0)
    for other in range(1, 4):
        earlier, unused = equal_counts(indices, other)
        product = product * (1.0 + earlier)
    return product


def contract_axis(tensor, pieces, position):
    others = [other for other in range(4) if other != position]
    leading = others[0]
    paired = (pieces[others[1]][:, None, :] * pieces[others[2]][None, :, :]).astype(jnp.bfloat16)
    kept = "".join(sorted(letters[position] + letters[leading]))
    pattern = "abcd," + letters[others[1]] + letters[others[2]] + "r->" + kept + "r"
    partial_sum = jnp.einsum(pattern, tensor, paired, preferred_element_type=jnp.float32)
    if position < leading:
        return jnp.sum(partial_sum * pieces[leading][None, :, :], axis=1)
    return jnp.sum(partial_sum * pieces[leading][:, None, :], axis=0)


def apply_tensor(tensor_blocks, block_index, current):
    tile_size = tensor_blocks.shape[1]
    blocks_count = NSIZE // tile_size
    total = jnp.zeros(current.shape, jnp.float32)
    for slot_id in range(tensor_blocks.shape[0]):
        tensor = tensor_blocks[slot_id].reshape(tile_size, tile_size, tile_size, tile_size)
        indices = block_index[slot_id]
        live = (indices[0] < blocks_count).astype(jnp.float32)
        safe = jnp.minimum(indices, blocks_count - 1)
        pieces = [
            lax.dynamic_slice_in_dim(current, safe[other] * tile_size, tile_size, 0)
            for other in range(4)
        ]
        weight = live * 6.0 / factor_product(indices)
        for position in range(4):
            result = weight * contract_axis(tensor, pieces, position)
            start = safe[position] * tile_size
            total = lax.dynamic_update_slice_in_dim(
                total, lax.dynamic_slice_in_dim(total, start, tile_size, 0) + result, start, 0
            )
    return total


def body(tensor_blocks, block_index, starts, shifts):
    own_count = starts.shape[1]
    offset = lax.axis_index(BLK) * own_count
    own_shifts = lax.dynamic_slice_in_dim(shifts, offset, own_count, 0)
    current_own = normalize(starts)
    current = gather_axes(current_own, (("blk_0", "blk_1"), ("blk_2", "blk_3")), 1)
    previous_own = current_own
    image_own = current_own
    for step_id in range(ITERS):
        applied = apply_tensor(tensor_blocks, block_index, current)
        final_turn = step_id == ITERS - 1
        summed = sum_by_parts(applied, (("blk_0", "blk_1"), ("blk_2", "blk_3")))
        image_own = lax.dynamic_slice_in_dim(summed, offset, own_count, 1)
        previous_own = lax.dynamic_slice_in_dim(current, offset, own_count, 1)
        if final_turn:
            current_own = normalize(image_own + own_shifts[None, :] * previous_own)
        else:
            current = normalize(summed + shifts[None, :] * current)
    estimate = jnp.mean(previous_own * image_own, axis=0) * lax.rsqrt(
        jnp.mean(image_own * image_own, axis=0) + 1e-06
    )
    return (current_own, estimate)


def solution(mesh):
    torus = Mesh(mesh.devices.reshape(4, 8, 4, 2), ("blk_0", "blk_1", "blk_2", "blk_3"))
    in_specs = (P(BLK, None, None, None), P(BLK, None), P(None, BLK), P())
    out_specs = (P(None, BLK), P(BLK))
    return jax.shard_map(body, mesh=torus, in_specs=in_specs, out_specs=out_specs, check_vma=False)
```

profile of v0, /device:TPU:1, one launch (start us, length us, event | category | flops | bytes accessed | tf_op | source)
XLA Modules:
  0.0 242.2 jit_solution(9051432041461809612)
XLA Ops:
  3.9 12.0 %all-to-all-start = ((f32[32,256,1]{1,2,0:T(1,128)}), f32[32,256,1]{1,2,0:T(1,128)S(1)}, u32[]{:S(2)}, u32[]{:S(2)}) async-start(f32[32,256,1]{1,2,0:T(1,128)} %broadcast_in_dim.21), calls=%async_computation | async-start | bytes 65536 | tf_op jit(solution)/shard_map/all_to_all | solution.py:17
  41.0 5.3 %all-to-all-start.1 = ((f32[8,32,256,1]{2,1,3,0:T(8,128)}), f32[8,32,256,1]{2,1,3,0:T(8,128)S(1)}, u32[]{:S(2)}, u32[]{:S(2)}) async-start(f32[8,32,256,1]{2,1,3,0:T(8,128)} %broadcast_in_dim.23), calls=%async_computation.1 | async-start | bytes 524288 | tf_op jit(solution)/shard_map/all_to_all | solution.py:17
  50.5 10.9 %reshape_squeeze.9 = bf16[32,32,32,32]{3,2,1,0:T(8,128)(2,1)} reshape(bf16[1,32,32,1024]{3,2,1,0:T(8,128)(2,1)} %get-tuple-element.16) | data formatting | bytes 4194304 | tf_op jit(solution)/shard_map/reshape;squeeze | solution.py:105
  61.4 8.1 %reshape_squeeze.8 = bf16[32,32,32,32]{3,2,1,0:T(8,128)(2,1)} reshape(bf16[1,32,32,1024]{3,2,1,0:T(8,128)(2,1)S(1)} %get-tuple-element.17) | data formatting | bytes 4194304 | tf_op jit(solution)/shard_map/reshape;squeeze | solution.py:105
  70.5 5.9 %fusion.34 = f32[32,256]{1,0:T(8,128)S(1)} fusion(bf16[32,32,32,32]{3,2,1,0:T(8,128)(2,1)} %reshape_squeeze.8, f32[32,256]{1,0:T(8,128)S(1)} %copy.121, f32[32,256]{1,0:T(8,128)S(1)} %copy.124, f32[32,256]{1,0:T(8,128)S(1)} %copy.125), kind=kOutput, calls=%fused_computation.34 | convolution fusion | flops 537911296 | bytes 2228224 | tf_op jit(solution)/shard_map/abcd,bcr->adr/dot_general | solution.py:94
  79.0 5.1 %multiply_reduce_fusion.6 = (f32[32,256]{1,0:T(8,128)S(1)}, f32[32,256]{1,0:T(8,128)S(1)}) fusion(f32[32,256]{1,0:T(8,128)S(1)} %copy.125, f32[32,256]{1,0:T(8,128)S(1)} %copy.124, bf16[32,32,32,32]{3,2,1,0:T(8,128)(2,1)S(1)} %copy-done, f32[32,256]{1,0:T(8,128)S(1)} %copy.122, f32[32,256]{1,0:T(8,128)S(1)} %copy.121), kind=kOutput, calls=%fused_computation.53 | convolution fusion | flops 538427392 | bytes 2293760 | tf_op jit(solution)/shard_map/abcd,cdr->abr/dot_general | solution.py:94
  84.4 5.3 %fusion.33 = f32[32,256]{1,0:T(8,128)S(1)} fusion(bf16[32,32,32,32]{3,2,1,0:T(8,128)(2,1)} %reshape_squeeze.9, f32[32,256]{1,0:T(8,128)S(1)} %copy.132, f32[32,256]{1,0:T(8,128)S(1)} %copy.133, f32[32,256]{1,0:T(8,128)S(1)} %copy.130), kind=kOutput, calls=%fused_computation.33 | convolution fusion | flops 537911296 | bytes 2228224 | tf_op jit(solution)/shard_map/abcd,bdr->acr/dot_general | solution.py:94
  89.7 7.2 %multiply_reduce_fusion.4 = (f32[32,256]{1,0:T(8,128)S(1)}, f32[32,256]{1,0:T(8,128)S(1)}) fusion(f32[32,256]{1,0:T(8,128)S(1)} %copy.133, f32[32,256]{1,0:T(8,128)S(1)} %copy.132, bf16[32,32,32,32]{3,2,1,0:T(8,128)(2,1)} %reshape_squeeze.9, f32[32,256]{1,0:T(8,128)S(1)} %copy.130, f32[32,256]{1,0:T(8,128)S(1)} %copy.129), kind=kOutput, calls=%fused_computation.48 | convolution fusion | flops 538427392 | bytes 2293760 | tf_op jit(solution)/shard_map/abcd,cdr->abr/dot_general | solution.py:94
  99.6 11.1 %all_to_all.52 = f32[8,32,1,256]{3,1,2,0:T(8,128)S(1)} all-to-all(f32[8,32,1,256]{3,1,2,0:T(8,128)S(1)} %copy.137), channel_id=1, replica_groups=mesh['blk_0'=4,'blk_1'=8,'blk_2'=4,'blk_3'=2] {'blk_2','blk_3'}, dimensions={0} | all-to-all | bytes 524288 | tf_op jit(solution)/shard_map/all_to_all | solution.py:46
  110.7 18.1 %all_to_all.53 = f32[32,1,256]{2,1,0:T(1,128)S(1)} all-to-all(f32[32,1,256]{2,1,0:T(1,128)S(1)} %reduce_sum.239), channel_id=1, replica_groups=mesh['blk_0'=4,'blk_1'=8,'blk_2'=4,'blk_3'=2] {'blk_0','blk_1'}, dimensions={0} | all-to-all | bytes 65536 | tf_op jit(solution)/shard_map/all_to_all | solution.py:54
  128.9 11.7 %all_to_all.50 = f32[32,1,256]{2,1,0:T(1,128)S(1)} all-to-all(f32[32,1,256]{2,1,0:T(1,128)S(1)} %broadcast_in_dim.24), channel_id=1, replica_groups=mesh['blk_0'=4,'blk_1'=8,'blk_2'=4,'blk_3'=2] {'blk_0','blk_1'}, dimensions={0} | all-to-all | bytes 65536 | tf_op jit(solution)/shard_map/all_to_all | solution.py:17
  141.3 6.9 %all-to-all-start.5 = ((f32[8,32,1,256]{3,1,2,0:T(8,128)}), f32[8,32,1,256]{3,1,2,0:T(8,128)S(1)}, u32[]{:S(2)}, u32[]{:S(2)}) async-start(f32[8,32,1,256]{3,1,2,0:T(8,128)} %broadcast_in_dim.26), calls=%async_computation.5 | async-start | bytes 524288 | tf_op jit(solution)/shard_map/all_to_all | solution.py:17
  148.3 6.4 %all-to-all-done.5 = f32[8,32,1,256]{3,1,2,0:T(8,128)S(1)} async-done(((f32[8,32,1,256]{3,1,2,0:T(8,128)}), f32[8,32,1,256]{3,1,2,0:T(8,128)S(1)}, u32[]{:S(2)}, u32[]{:S(2)}) %all-to-all-start.5) | async-done | bytes 262176 | tf_op jit(solution)/shard_map/all_to_all | solution.py:17
  156.0 5.9 %fusion.28 = f32[32,256]{1,0:T(8,128)S(1)} fusion(bf16[32,32,32,32]{3,2,1,0:T(8,128)(2,1)} %reshape_squeeze.9, f32[32,256]{1,0:T(8,128)S(1)} %copy.149, f32[32,256]{1,0:T(8,128)S(1)} %copy.152, f32[32,256]{1,0:T(8,128)S(1)} %copy.153), kind=kOutput, calls=%fused_computation.28 | convolution fusion | flops 537911296 | bytes 2228224 | tf_op jit(solution)/shard_map/abcd,bcr->adr/dot_general | solution.py:94
  161.9 5.5 %fusion.29 = f32[32,256]{1,0:T(8,128)S(1)} fusion(bf16[32,32,32,32]{3,2,1,0:T(8,128)(2,1)} %reshape_squeeze.9, f32[32,256]{1,0:T(8,128)S(1)} %copy.152, f32[32,256]{1,0:T(8,128)S(1)} %copy.153, f32[32,256]{1,0:T(8,128)S(1)} %copy.150), kind=kOutput, calls=%fused_computation.29 | convolution fusion | flops 537911296 | bytes 2228224 | tf_op jit(solution)/shard_map/abcd,bdr->acr/dot_general | solution.py:94
  167.5 5.1 %multiply_reduce_fusion = (f32[32,256]{1,0:T(8,128)S(1)}, f32[32,256]{1,0:T(8,128)S(1)}) fusion(f32[32,256]{1,0:T(8,128)S(1)} %copy.153, f32[32,256]{1,0:T(8,128)S(1)} %copy.152, bf16[32,32,32,32]{3,2,1,0:T(8,128)(2,1)S(1)} %bitcast.251, f32[32,256]{1,0:T(8,128)S(1)} %copy.150, f32[32,256]{1,0:T(8,128)S(1)} %copy.149), kind=kOutput, calls=%fused_computation.38 | convolution fusion | flops 538427392 | bytes 2293760 | tf_op jit(solution)/shard_map/abcd,cdr->abr/dot_general | solution.py:94
  172.8 5.9 %fusion.30 = f32[32,256]{1,0:T(8,128)S(1)} fusion(bf16[32,32,32,32]{3,2,1,0:T(8,128)(2,1)} %reshape_squeeze.8, f32[32,256]{1,0:T(8,128)S(1)} %copy.141, f32[32,256]{1,0:T(8,128)S(1)} %copy.144, f32[32,256]{1,0:T(8,128)S(1)} %copy.145), kind=kOutput, calls=%fused_computation.30 | convolution fusion | flops 537911296 | bytes 2228224 | tf_op jit(solution)/shard_map/abcd,bcr->adr/dot_general | solution.py:94
  178.8 5.3 %fusion.31 = f32[32,256]{1,0:T(8,128)S(1)} fusion(bf16[32,32,32,32]{3,2,1,0:T(8,128)(2,1)} %reshape_squeeze.8, f32[32,256]{1,0:T(8,128)S(1)} %copy.144, f32[32,256]{1,0:T(8,128)S(1)} %copy.145, f32[32,256]{1,0:T(8,128)S(1)} %copy.142), kind=kOutput, calls=%fused_computation.31 | convolution fusion | flops 537911296 | bytes 2228224 | tf_op jit(solution)/shard_map/abcd,bdr->acr/dot_general | solution.py:94
  184.0 5.1 %multiply_reduce_fusion.2 = (f32[32,256]{1,0:T(8,128)S(1)}, f32[32,256]{1,0:T(8,128)S(1)}) fusion(f32[32,256]{1,0:T(8,128)S(1)} %copy.145, f32[32,256]{1,0:T(8,128)S(1)} %copy.144, bf16[32,32,32,32]{3,2,1,0:T(8,128)(2,1)S(1)} %bitcast.247, f32[32,256]{1,0:T(8,128)S(1)} %copy.142, f32[32,256]{1,0:T(8,128)S(1)} %copy.141), kind=kOutput, calls=%fused_computation.43 | convolution fusion | flops 538427392 | bytes 2293760 | tf_op jit(solution)/shard_map/abcd,cdr->abr/dot_general | solution.py:94
  189.4 9.9 %all_to_all.54 = f32[8,32,1,256]{3,1,2,0:T(8,128)S(1)} all-to-all(f32[8,32,1,256]{3,1,2,0:T(8,128)S(1)} %copy.157), channel_id=1, replica_groups=mesh['blk_0'=4,'blk_1'=8,'blk_2'=4,'blk_3'=2] {'blk_2','blk_3'}, dimensions={0} | all-to-all | bytes 524288 | tf_op jit(solution)/shard_map/all_to_all | solution.py:46
  199.4 11.7 %all_to_all.55 = f32[32,1,256]{2,1,0:T(1,128)S(1)} all-to-all(f32[32,1,256]{2,1,0:T(1,128)S(1)} %reduce_sum.251), channel_id=1, replica_groups=mesh['blk_0'=4,'blk_1'=8,'blk_2'=4,'blk_3'=2] {'blk_0','blk_1'}, dimensions={0} | all-to-all | bytes 65536 | tf_op jit(solution)/shard_map/all_to_all | solution.py:54
  211.1 11.7 %all_to_all.51 = f32[32,1,256]{2,1,0:T(1,128)S(1)} all-to-all(f32[32,1,256]{2,1,0:T(1,128)S(1)} %broadcast_in_dim.27), channel_id=1, replica_groups=mesh['blk_0'=4,'blk_1'=8,'blk_2'=4,'blk_3'=2] {'blk_0','blk_1'}, dimensions={0} | all-to-all | bytes 65536 | tf_op jit(solution)/shard_map/all_to_all | solution.py:17
  223.5 6.6 %all-to-all-start.9 = ((f32[8,32,1,256]{3,1,2,0:T(8,128)}), f32[8,32,1,256]{3,1,2,0:T(8,128)S(1)}, u32[]{:S(2)}, u32[]{:S(2)}) async-start(f32[8,32,1,256]{3,1,2,0:T(8,128)} %broadcast_in_dim.29), calls=%async_computation.9 | async-start | bytes 524288 | tf_op jit(solution)/shard_map/all_to_all | solution.py:17
  230.8 5.9 %all-to-all-done.9 = f32[8,32,1,256]{3,1,2,0:T(8,128)S(1)} async-done(((f32[8,32,1,256]{3,1,2,0:T(8,128)}), f32[8,32,1,256]{3,1,2,0:T(8,128)S(1)}, u32[]{:S(2)}, u32[]{:S(2)}) %all-to-all-start.9) | async-done | bytes 262176 | tf_op jit(solution)/shard_map/all_to_all | solution.py:17
  (95 shorter events, 23.4 us)
Async XLA Ops:
  3.9 36.3 %all-to-all-start = ((f32[32,256,1]{1,2,0:T(1,128)}), f32[32,256,1]{1,2,0:T(1,128)S(1)}, u32[]{:S(2)}, u32[]{:S(2)}) async-start(f32[32,256,1]{1,2,0:T(1,128)} %broadcast_in_dim.21), calls=%async_computation | async-start | bytes 65536 | tf_op jit(solution)/shard_map/all_to_all | solution.py:17
  41.0 28.7 %all-to-all-start.1 = ((f32[8,32,256,1]{2,1,3,0:T(8,128)}), f32[8,32,256,1]{2,1,3,0:T(8,128)S(1)}, u32[]{:S(2)}, u32[]{:S(2)}) async-start(f32[8,32,256,1]{2,1,3,0:T(8,128)} %broadcast_in_dim.23), calls=%async_computation.1 | async-start | bytes 524288 | tf_op jit(solution)/shard_map/all_to_all | solution.py:17
  70.5 5.9 %copy-start = (bf16[32,32,32,32]{3,2,1,0:T(8,128)(2,1)S(1)}, bf16[32,32,32,32]{3,2,1,0:T(8,128)(2,1)}, u32[]{:S(2)}) copy-start(bf16[32,32,32,32]{3,2,1,0:T(8,128)(2,1)} %reshape_squeeze.8) | copy-start | bytes 6291460
  84.4 12.5 %slice-start.2 = ((s8[8388608]{0:T(1024)(128)(4,1)}), s8[4194304]{0:T(1024)(128)(4,1)S(1)}, s32[]{:S(2)}) async-start(s8[8388608]{0:T(1024)(128)(4,1)} %bitcast.248), calls=%async_computation.12 | async-start | bytes 8388608
  89.7 7.2 %slice-start.3 = ((s8[8388608]{0:T(1024)(128)(4,1)}), s8[4194304]{0:T(1024)(128)(4,1)S(1)}, s32[]{:S(2)}) async-start(s8[8388608]{0:T(1024)(128)(4,1)} %bitcast.248), calls=%async_computation.13 | async-start | bytes 8388608
  96.9 57.8 %copy-start.1 = (f32[256]{0:T(256)S(1)}, f32[256]{0:T(256)}, u32[]{:S(2)}) copy-start(f32[256]{0:T(256)} %param.7) | copy-start | bytes 3076
  141.3 13.4 %all-to-all-start.5 = ((f32[8,32,1,256]{3,1,2,0:T(8,128)}), f32[8,32,1,256]{3,1,2,0:T(8,128)S(1)}, u32[]{:S(2)}, u32[]{:S(2)}) async-start(f32[8,32,1,256]{3,1,2,0:T(8,128)} %broadcast_in_dim.26), calls=%async_computation.5 | async-start | bytes 524288 | tf_op jit(solution)/shard_map/all_to_all | solution.py:17
  156.0 11.4 %slice-start.4 = ((s8[8388608]{0:T(1024)(128)(4,1)}), s8[4194304]{0:T(1024)(128)(4,1)S(1)}, s32[]{:S(2)}) async-start(s8[8388608]{0:T(1024)(128)(4,1)} %bitcast.250), calls=%async_computation.14 | async-start | bytes 8388608
  161.9 5.5 %slice-start.5 = ((s8[8388608]{0:T(1024)(128)(4,1)}), s8[4194304]{0:T(1024)(128)(4,1)S(1)}, s32[]{:S(2)}) async-start(s8[8388608]{0:T(1024)(128)(4,1)} %bitcast.250), calls=%async_computation.15 | async-start | bytes 8388608
  172.8 11.2 %slice-start = ((s8[8388608]{0:T(1024)(128)(4,1)}), s8[4194304]{0:T(1024)(128)(4,1)S(1)}, s32[]{:S(2)}) async-start(s8[8388608]{0:T(1024)(128)(4,1)} %bitcast.246), calls=%async_computation.10 | async-start | bytes 8388608
  178.7 5.3 %slice-start.1 = ((s8[8388608]{0:T(1024)(128)(4,1)}), s8[4194304]{0:T(1024)(128)(4,1)S(1)}, s32[]{:S(2)}) async-start(s8[8388608]{0:T(1024)(128)(4,1)} %bitcast.246), calls=%async_computation.11 | async-start | bytes 8388608
  223.5 13.1 %all-to-all-start.9 = ((f32[8,32,1,256]{3,1,2,0:T(8,128)}), f32[8,32,1,256]{3,1,2,0:T(8,128)S(1)}, u32[]{:S(2)}, u32[]{:S(2)}) async-start(f32[8,32,1,256]{3,1,2,0:T(8,128)} %broadcast_in_dim.29), calls=%async_computation.9 | async-start | bytes 524288 | tf_op jit(solution)/shard_map/all_to_all | solution.py:17
where the time goes:
time: 247 us; the launch traced here: 242 us
  blocking collectives  74.1 us (30%)
  matrix products  61.1 us (25%)
  local copies, waits for them, and re-layouts  32.1 us (13%)
  starting transfers between devices  30.8 us (12%)
  between operations  26.5 us (11%)
  waiting for transfers between devices  12.3 us (5%)
  other arithmetic  5.36 us (2%)
    dot_general x12, matrix products, contract_axis(): jnp.einsum(pattern, tensor, paired, preferred_element_type=jnp.float32)  61.1 us
    all_to_all x4, starting transfers between devices, from_everyone(): lax.all_to_all(jnp.broadcast_to(x[None], (count, *x.shape)), axis, 0, 0,...  30.8 us
    all_to_all x2, blocking collectives, summed_rows(): lax.all_to_all(nearer, far, split_axis=0, concat_axis=0, tiled=True)  29.7 us
    all_to_all x2, blocking collectives, from_everyone(): lax.all_to_all(jnp.broadcast_to(x[None], (count, *x.shape)), axis, 0, 0,...  23.4 us
    all_to_all x2, blocking collectives, summed_on_arrival(): blocks = lax.all_to_all(cut_along(x, dim, count), axis, 0, 0, tiled=True)  21 us
    another operation x2, local copies, waits for them, and re-layouts, apply_tensor(): tensor_blocks[slot_id].reshape(tile_size, tile_size, tile_size, tile_size)  19 us
    all_to_all x4, waiting for transfers between devices, from_everyone(): lax.all_to_all(jnp.broadcast_to(x[None], (count, *x.shape)), axis, 0, 0,...  12.3 us
  transfers between devices with their start and end apart: 4, of which 2 were waited for; matrix products, arithmetic and copies ran while one was open for 11% of the time, Pallas kernels for 0%

commit v1 on v0

v1 whole, which is shorter than its diff:
```python
import functools

import jax
import jax.numpy as jnp
from jax import lax
from jax.experimental import pallas as pl
from jax.experimental.pallas import tpu as pltpu
from jax.sharding import Mesh
from jax.sharding import PartitionSpec as P

BLK = ("y", "z", "x", "c")
TORUS = (4, 8, 4, 2)
MESH = pl.DeviceIdType.MESH
EPS = 1e-06


def normalized(values):
    return values * lax.rsqrt(jnp.mean(values * values, axis=0, keepdims=True) + EPS)


def slot_weight(idx, blocks_count):
    weight = jnp.where(idx[0] < blocks_count, 6.0, 0.0)
    for other in range(1, 4):
        earlier = jnp.zeros(idx[0].shape, jnp.int32)
        for before in range(other):
            earlier = earlier + jnp.where(idx[before] == idx[other], 1, 0)
        share = jnp.ones(idx[0].shape, jnp.float32)
        for count in range(1, other + 1):
            share = jnp.where(earlier == count, 1.0 / (1 + count), share)
        weight = weight * share
    return weight


def kernel(
    sizes,
    torus,
    bi_ref,
    shifts_sref,
    shifts_ref,
    starts_ref,
    tensor_ref,
    out_ref,
    est_ref,
    mats,
    pair,
    cur,
    pieces,
    ybuf,
    total,
    zrows,
    ztile,
    cols,
    arrived,
    zsums,
    zpart,
    zparts,
    image,
    flipped,
    arrived2,
    zsend,
    zlast,
    send_sem,
    recv_sem,
    load_sem,
):
    slots, bs, nsize, starts = sizes
    ny, nz, nx, nc = torus
    group = ny * nx * nc
    blocks_count = nsize // bs
    piece = nsize // group
    y, z, x, c = (lax.axis_index(name) for name in BLK)
    me = (y * nx + x) * nc + c

    loads = []
    for s in range(slots):
        load = pltpu.make_async_copy(tensor_ref.at[s], mats.at[2 * s], load_sem.at[s])
        load.start()
        loads.append(load)

    plane = []
    for dy in range(ny):
        for dx in range(nx):
            for dc in range(nc):
                if dy or dx or dc:
                    py = lax.rem(y + dy, ny)
                    px = lax.rem(x + dx, nx)
                    pc = lax.rem(c + dc, nc)
                    plane.append(((py, z, px, pc), (py * nx + px) * nc + pc))
    line = []
    for dz in range(1, nz):
        pz = lax.rem(z + dz, nz)
        line.append(((y, pz, x, c), pz))

    barrier = pltpu.get_barrier_semaphore()
    for peer, _ in plane + line:
        pl.semaphore_signal(barrier, inc=1, device_id=peer, device_id_type=MESH)
    pl.semaphore_wait(barrier, len(plane) + len(line))

    def send(phase, src, dst, peer):
        pltpu.make_async_remote_copy(
            src_ref=src,
            dst_ref=dst,
            send_sem=send_sem.at[phase],
            recv_sem=recv_sem.at[phase],
            device_id=peer,
            device_id_type=MESH,
        ).start()

    def wait(sem, span):
        pltpu.make_async_copy(span, span, sem).wait()

    for peer, _ in line:
        send(0, starts_ref, zrows.at[z], peer)
    own = pltpu.make_async_copy(starts_ref, zrows.at[z], load_sem.at[slots])
    own.start()

    def flip(s):
        loads[s].wait()
        side = bs * bs
        step = min(side, 256)
        for i in range(0, side, step):
            for j in range(0, side, step):
                tile = mats[2 * s, i : i + step, j : j + step]
                mats[2 * s + 1, j : j + step, i : i + step] = tile.T

    held = lax.broadcasted_iota(jnp.int32, (starts, starts), 1)
    given = lax.broadcasted_iota(jnp.int32, (starts, starts), 0)
    hz = held % nz
    hc = (held // nz) % nc
    hx = (held // (nz * nc)) % nx
    hy = held // (nz * nc * nx)
    where_from = ((hy * nz + hz) * nx + hx) * nc + hc
    chosen = jnp.where(given == where_from, 1.0, 0.0).astype(jnp.float32)
    shifts = jnp.dot(
        jnp.broadcast_to(shifts_ref[...], (8, starts)),
        chosen,
        precision=lax.Precision.HIGHEST,
        preferred_element_type=jnp.float32,
    )[0:1, :]

    own.wait()
    wait(recv_sem.at[0], zrows.at[pl.ds(0, nz - 1)])
    ztile[...] = zrows[...].reshape(nz, nsize)
    for peer, _ in plane:
        send(1, ztile, cols.at[me], peer)
    for s in range(slots):
        flip(s)
    wait(recv_sem.at[1], cols.at[pl.ds(0, group - 1)])
    cols[me] = ztile[...]
    cur[0] = normalized(cols[...].reshape(starts, nsize).T)

    def index(s, position):
        return bi_ref[s : s + 1, position : position + 1]

    def spot(s, position):
        safe = jnp.minimum(index(s, position), blocks_count - 1)
        return jnp.broadcast_to(safe, (bs, starts))

    def contract(turn):
        for s in range(slots):
            for position in range(4):
                at = spot(s, position)
                rows = cur[turn, 0:bs, :]
                for p in range(1, blocks_count):
                    rows = jnp.where(at == p, cur[turn, p * bs : (p + 1) * bs, :], rows)
                pieces[4 * s + position] = rows

        def one(q, carry):
            s = q // 2
            m = q % 2
            side = bs * bs

            def rows(position):
                return pieces[4 * s + position]

            first, second = rows(2 - 2 * m), rows(3 - 2 * m)
            for a in range(bs):
                pair[a * bs : (a + 1) * bs, :] = (first[a : a + 1, :] * second).astype(
                    jnp.bfloat16
                )
            lead, trail = rows(2 * m), rows(2 * m + 1)
            down = jnp.zeros((bs, starts), jnp.float32)
            per = min(bs, 8)
            for t in range(0, bs, per):
                part = jnp.dot(
                    mats[q, t * bs : (t + per) * bs, :],
                    pair[...],
                    preferred_element_type=jnp.float32,
                ).reshape(per, bs, starts)
                ybuf[2 * q, t : t + per, :] = jnp.sum(part * trail[None], axis=1)
                for a in range(per):
                    down = down + part[a] * lead[t + a : t + a + 1, :]
            ybuf[2 * q + 1] = down
            return carry

        lax.fori_loop(0, 2 * slots, one, 0)
        sums = [jnp.zeros((bs, starts), jnp.float32) for _ in range(blocks_count)]
        for s in range(slots):
            weight = slot_weight([index(s, position) for position in range(4)], blocks_count)
            for position in range(4):
                part = ybuf[4 * s + position] * weight
                at = spot(s, position)
                for p in range(blocks_count):
                    sums[p] = sums[p] + jnp.where(at == p, part, 0.0)
        return sums

    sums = contract(0)
    for p in range(blocks_count):
        total[p * bs : (p + 1) * bs, :] = sums[p]
    for peer, other in plane:
        send(2, total.at[pl.ds(pl.multiple_of(other * piece, piece), piece)], arrived.at[me], peer)
    arrived[me] = total[pl.ds(pl.multiple_of(me * piece, piece), piece), :]
    wait(recv_sem.at[2], arrived.at[pl.ds(0, group - 1)])
    zpart[...] = jnp.sum(arrived[...], axis=0)
    for peer, _ in line:
        send(3, zpart, zparts.at[z], peer)
    zparts[z] = zpart[...]
    wait(recv_sem.at[3], zparts.at[pl.ds(0, nz - 1)])
    zsums[...] = jnp.sum(zparts[...], axis=0)
    for peer, _ in plane:
        send(4, zsums, image.at[me], peer)
    image[me] = zsums[...]
    wait(recv_sem.at[4], image.at[pl.ds(0, group - 1)])
    cur[1] = normalized(image[...].reshape(nsize, starts) + shifts * cur[0])

    sums = contract(1)
    for p in range(blocks_count):
        flipped[:, p * bs : (p + 1) * bs] = sums[p].T
    for peer, other in plane:
        send(5, flipped.at[pl.ds(pl.multiple_of(other * nz, nz), nz)], arrived2.at[me], peer)
    arrived2[me] = flipped[pl.ds(pl.multiple_of(me * nz, nz), nz), :]
    cols[...] = cur[1].T.reshape(group, nz, nsize)
    wait(recv_sem.at[5], arrived2.at[pl.ds(0, group - 1)])
    zsend[...] = jnp.sum(arrived2[...], axis=0).reshape(nz, 1, nsize)
    for peer, other in line:
        send(6, zsend.at[other], zlast.at[z], peer)
    zlast[z] = zsend[z]
    previous = cols[me, pl.ds(z, 1), :]
    own_shift = shifts_sref[((y * nz + z) * nx + x) * nc + c]
    wait(recv_sem.at[6], zlast.at[pl.ds(0, nz - 1)])
    mine = jnp.sum(zlast[...], axis=0)
    last = mine + own_shift * previous
    out_ref[...] = last * lax.rsqrt(jnp.mean(last * last, axis=1, keepdims=True) + EPS)
    scale = lax.rsqrt(jnp.mean(mine * mine, axis=1, keepdims=True) + EPS)
    est_ref[...] = jnp.mean(previous * mine, axis=1, keepdims=True) * scale

    spans = (zrows, cols, arrived, zparts, image, arrived2, zlast)
    for phase, span in enumerate(spans):
        wait(send_sem.at[phase], span.at[pl.ds(0, span.shape[0] - 1)])


def body(torus, tensor_blocks, block_index, starts, shifts):
    slots, bs = tensor_blocks.shape[:2]
    nsize = starts.shape[0]
    count = shifts.shape[0]
    ny, nz, nx, nc = torus
    group = ny * nx * nc
    piece = nsize // group
    side = bs * bs
    f32 = jnp.float32
    vmem, smem = pltpu.MemorySpace.VMEM, pltpu.MemorySpace.SMEM
    phases = 7
    iterate, estimate = pl.pallas_call(
        functools.partial(kernel, (slots, bs, nsize, count), torus),
        out_shape=(
            jax.ShapeDtypeStruct((1, nsize), f32),
            jax.ShapeDtypeStruct((1, 1), f32),
        ),
        in_specs=[
            pl.BlockSpec(memory_space=vmem),
            pl.BlockSpec(memory_space=smem),
            pl.BlockSpec(memory_space=vmem),
            pl.BlockSpec(memory_space=pl.ANY),
            pl.BlockSpec(memory_space=pl.ANY),
        ],
        out_specs=(pl.BlockSpec(memory_space=vmem), pl.BlockSpec(memory_space=vmem)),
        scratch_shapes=[
            pltpu.VMEM((2 * slots, side, side), jnp.bfloat16),
            pltpu.VMEM((side, count), jnp.bfloat16),
            pltpu.VMEM((2, nsize, count), f32),
            pltpu.VMEM((4 * slots, bs, count), f32),
            pltpu.VMEM((4 * slots, bs, count), f32),
            pltpu.VMEM((nsize, count), f32),
            pltpu.VMEM((nz, 1, nsize), f32),
            pltpu.VMEM((nz, nsize), f32),
            pltpu.VMEM((group, nz, nsize), f32),
            pltpu.VMEM((group, piece, count), f32),
            pltpu.VMEM((piece, count), f32),
            pltpu.VMEM((piece, count), f32),
            pltpu.VMEM((nz, piece, count), f32),
            pltpu.VMEM((group, piece, count), f32),
            pltpu.VMEM((count, nsize), f32),
            pltpu.VMEM((group, nz, nsize), f32),
            pltpu.VMEM((nz, 1, nsize), f32),
            pltpu.VMEM((nz, 1, nsize), f32),
            pltpu.SemaphoreType.DMA((phases,)),
            pltpu.SemaphoreType.DMA((phases,)),
            pltpu.SemaphoreType.DMA((slots + 1,)),
        ],
        compiler_params=pltpu.CompilerParams(collective_id=0, has_side_effects=True),
        name="power",
    )(
        block_index,
        shifts,
        shifts.reshape(1, count),
        starts.reshape(1, nsize),
        tensor_blocks.reshape(slots, side, side),
    )
    return iterate.reshape(nsize, 1), estimate.reshape(1)


def solution(mesh):
    torus = Mesh(mesh.devices.reshape(TORUS), BLK)
    in_specs = (P(BLK, None, None, None), P(BLK, None), P(None, BLK), P())
    out_specs = (P(None, BLK), P(BLK))
    return jax.shard_map(
        functools.partial(body, TORUS), mesh=torus, in_specs=in_specs, out_specs=out_specs, check_vma=False
    )
```

time: 247 us -> 61.9 us (0.25); the launches traced: 242 us -> 61.7 us
  blocking collectives: 74.1 us -> 0 us
  matrix products: 61.1 us -> 0 us
  Pallas kernels: 0 us -> 58.1 us
  local copies, waits for them, and re-layouts: 32.1 us -> 1.22 us
  starting transfers between devices: 30.8 us -> 0 us
  between operations: 26.5 us -> 2.4 us
  waiting for transfers between devices: 12.3 us -> 0 us
  other arithmetic: 5.36 us -> 0 us
    all_to_all x6 -> x0, blocking collectives: 74.1 us -> none  [the longest x2 29.7 us: summed_rows(): lax.all_to_all(nearer, far, split_axis=0, concat_axis=0, tiled=True)]
    dot_general x12 -> x0, matrix products: 61.1 us -> none  [contract_axis(): jnp.einsum(pattern, tensor, paired, preferred_element_type=jnp.float32)]
    pallas_call x0 -> x1, Pallas kernels: none -> 58.1 us  [body(): pl.pallas_call(functools.partial(kernel, (slots, bs, nsize, count), torus...]
    all_to_all x4 -> x0, starting transfers between devices: 30.8 us -> none  [from_everyone(): lax.all_to_all(jnp.broadcast_to(x[None], (count, *x.shape)), axis, 0, 0,...]
    another operation x5 -> x0, local copies, waits for them, and re-layouts: 19.2 us -> none  [the longest x2 19 us: apply_tensor(): tensor_blocks[slot_id].reshape(tile_size, tile_size, tile_size, tile_size)]
    all_to_all x4 -> x0, waiting for transfers between devices: 12.3 us -> none  [from_everyone(): lax.all_to_all(jnp.broadcast_to(x[None], (count, *x.shape)), axis, 0, 0,...]
    slice x3 -> x0, local copies, waits for them, and re-layouts: 6.61 us -> none  [the longest x1 4.27 us: apply_tensor(): tensor_blocks[slot_id].reshape(tile_size, tile_size, tile_size, tile_size)]
    reduce_sum x7 -> x0, other arithmetic: 2.96 us -> none  [the longest x2 1.46 us: normalize(): return values * lax.rsqrt(jnp.mean(values * values, axis=0) + 1e-06)]
  transfers between devices with their start and end apart: 4 -> 0, of which waited for: 2 -> 0; matrix products, arithmetic and copies ran while one was open for 11% -> 0% of each run, Pallas kernels for 0% -> 0%
where the time goes in v1:
time: 61.9 us; the launch traced here: 61.7 us
  Pallas kernels  58.1 us (94%)
  between operations  2.4 us (4%)
  local copies, waits for them, and re-layouts  1.22 us (2%)
    pallas_call x1, Pallas kernels, body(): pl.pallas_call(functools.partial(kernel, (slots, bs, nsize, count), torus...  58.1 us

profile of v1, /device:TPU:1, one launch (start us, length us, event | category | flops | bytes accessed | tf_op | source)
XLA Modules:
  0.0 61.7 jit_solution(15334968809372533798)
XLA Ops:
  0.6 58.1 %power.1 = (f32[1,256]{1,0:T(1,128)}, f32[1,1]{1,0:T(1,128)}) custom-call(s32[2,4]{1,0:T(2,128)} %bi_ref.1, f32[256]{0:T(256)} %shifts_sref.1, f32[1,256]{1,0:T(1,128)} %bitcast.6, f32[1,256]{1,0:T(1,128)} %bitcast.7, bf16[2,1024,1024]{2,1,0:T(8,128)(2,1)} %bitcast.5), custom_call_target="tpu_custom_call" | custom-call | tf_op jit(solution)/shard_map/power/pallas_call | solution.py:263
  58.8 1.2 %copy.8 = f32[256,1]{0,1:T(1,128)} copy(f32[256,1]{0,1:T(1,128)} %bitcast.8) | data formatting | bytes 2048

commit v2 on v1

--- a/solution.py
+++ b/solution.py
@@ -34,13 +34,11 @@
 def kernel(
     sizes,
     torus,
-    bi_ref,
-    shifts_sref,
-    shifts_ref,
+    bi_hbm,
+    shifts_hbm,
     starts_ref,
     tensor_ref,
     out_ref,
-    est_ref,
     mats,
     pair,
     cur,
@@ -59,6 +57,8 @@
     arrived2,
     zsend,
     zlast,
+    bi_ref,
+    shifts_ref,
     send_sem,
     recv_sem,
     load_sem,
@@ -71,6 +71,14 @@
     y, z, x, c = (lax.axis_index(name) for name in BLK)
     me = (y * nx + x) * nc + c
 
+    own = pltpu.make_async_copy(starts_ref, zrows.at[z], load_sem.at[slots])
+    own.start()
+    small = [
+        pltpu.make_async_copy(shifts_hbm, shifts_ref, load_sem.at[slots + 1]),
+        pltpu.make_async_copy(bi_hbm, bi_ref, load_sem.at[slots + 2]),
+    ]
+    for load in small:
+        load.start()
     loads = []
     for s in range(slots):
         load = pltpu.make_async_copy(tensor_ref.at[s], mats.at[2 * s], load_sem.at[s])
@@ -94,6 +102,7 @@
     barrier = pltpu.get_barrier_semaphore()
     for peer, _ in plane + line:
         pl.semaphore_signal(barrier, inc=1, device_id=peer, device_id_type=MESH)
+    own.wait()
     pl.semaphore_wait(barrier, len(plane) + len(line))
 
     def send(phase, src, dst, peer):
@@ -110,9 +119,7 @@
         pltpu.make_async_copy(span, span, sem).wait()
 
     for peer, _ in line:
-        send(0, starts_ref, zrows.at[z], peer)
-    own = pltpu.make_async_copy(starts_ref, zrows.at[z], load_sem.at[slots])
-    own.start()
+        send(0, zrows.at[z], zrows.at[z], peer)
 
     def flip(s):
         loads[s].wait()
@@ -123,6 +130,15 @@
                 tile = mats[2 * s, i : i + step, j : j + step]
                 mats[2 * s + 1, j : j + step, i : i + step] = tile.T
 
+    wait(recv_sem.at[0], zrows.at[pl.ds(0, nz - 1)])
+    ztile[...] = zrows[...].reshape(nz, nsize)
+    for peer, _ in plane:
+        send(1, ztile, cols.at[me], peer)
+    for load in small:
+        load.wait()
+    column = ((y * nz + z) * nx + x) * nc + c
+    lane = lax.broadcasted_iota(jnp.int32, (1, starts), 1)
+    own_shift = jnp.sum(jnp.where(lane == column, shifts_ref[...], 0.0), axis=1, keepdims=True)
     held = lax.broadcasted_iota(jnp.int32, (starts, starts), 1)
     given = lax.broadcasted_iota(jnp.int32, (starts, starts), 0)
     hz = held % nz
@@ -138,11 +154,6 @@
         preferred_element_type=jnp.float32,
     )[0:1, :]
 
-    own.wait()
-    wait(recv_sem.at[0], zrows.at[pl.ds(0, nz - 1)])
-    ztile[...] = zrows[...].reshape(nz, nsize)
-    for peer, _ in plane:
-        send(1, ztile, cols.at[me], peer)
     for s in range(slots):
         flip(s)
     wait(recv_sem.at[1], cols.at[pl.ds(0, group - 1)])
@@ -193,7 +204,7 @@
             ybuf[2 * q + 1] = down
             return carry
 
-        lax.fori_loop(0, 2 * slots, one, 0)
+        lax.fori_loop(0, 2 * slots, one, 0, unroll=True)
         sums = [jnp.zeros((bs, starts), jnp.float32) for _ in range(blocks_count)]
         for s in range(slots):
             weight = slot_weight([index(s, position) for position in range(4)], blocks_count)
@@ -236,17 +247,21 @@
         send(6, zsend.at[other], zlast.at[z], peer)
     zlast[z] = zsend[z]
     previous = cols[me, pl.ds(z, 1), :]
-    own_shift = shifts_sref[((y * nz + z) * nx + x) * nc + c]
     wait(recv_sem.at[6], zlast.at[pl.ds(0, nz - 1)])
     mine = jnp.sum(zlast[...], axis=0)
     last = mine + own_shift * previous
-    out_ref[...] = last * lax.rsqrt(jnp.mean(last * last, axis=1, keepdims=True) + EPS)
+    out_ref[0:1, :] = last * lax.rsqrt(jnp.mean(last * last, axis=1, keepdims=True) + EPS)
     scale = lax.rsqrt(jnp.mean(mine * mine, axis=1, keepdims=True) + EPS)
-    est_ref[...] = jnp.mean(previous * mine, axis=1, keepdims=True) * scale
+    out_ref[1:2, :] = previous * mine * (scale / nsize)
 
     spans = (zrows, cols, arrived, zparts, image, arrived2, zlast)
     for phase, span in enumerate(spans):
         wait(send_sem.at[phase], span.at[pl.ds(0, span.shape[0] - 1)])
+
+
+def tail(rows_ref, out_ref, est_ref):
+    out_ref[...] = rows_ref[0:1, :]
+    est_ref[...] = jnp.sum(rows_ref[1:2, :], axis=1, keepdims=True)
 
 
 def body(torus, tensor_blocks, block_index, starts, shifts):
@@ -258,22 +273,20 @@
     piece = nsize // group
     side = bs * bs
     f32 = jnp.float32
-    vmem, smem = pltpu.MemorySpace.VMEM, pltpu.MemorySpace.SMEM
+    vmem = pltpu.MemorySpace.VMEM
     phases = 7
-    iterate, estimate = pl.pallas_call(
+    (rows,) = pl.pallas_call(
         functools.partial(kernel, (slots, bs, nsize, count), torus),
         out_shape=(
-            jax.ShapeDtypeStruct((1, nsize), f32),
-            jax.ShapeDtypeStruct((1, 1), f32),
+            jax.ShapeDtypeStruct((2, nsize), f32),
         ),
         in_specs=[
-            pl.BlockSpec(memory_space=vmem),
-            pl.BlockSpec(memory_space=smem),
-            pl.BlockSpec(memory_space=vmem),
+            pl.BlockSpec(memory_space=pl.ANY),
+            pl.BlockSpec(memory_space=pl.ANY),
             pl.BlockSpec(memory_space=pl.ANY),
             pl.BlockSpec(memory_space=pl.ANY),
         ],
-        out_specs=(pl.BlockSpec(memory_space=vmem), pl.BlockSpec(memory_space=vmem)),
+        out_specs=(pl.BlockSpec(memory_space=vmem),),
         scratch_shapes=[
             pltpu.VMEM((2 * slots, side, side), jnp.bfloat16),
             pltpu.VMEM((side, count), jnp.bfloat16),
@@ -293,19 +306,28 @@
             pltpu.VMEM((group, nz, nsize), f32),
             pltpu.VMEM((nz, 1, nsize), f32),
             pltpu.VMEM((nz, 1, nsize), f32),
+            pltpu.VMEM(block_index.shape, jnp.int32),
+            pltpu.VMEM((1, count), f32),
             pltpu.SemaphoreType.DMA((phases,)),
             pltpu.SemaphoreType.DMA((phases,)),
-            pltpu.SemaphoreType.DMA((slots + 1,)),
+            pltpu.SemaphoreType.DMA((slots + 3,)),
         ],
         compiler_params=pltpu.CompilerParams(collective_id=0, has_side_effects=True),
         name="power",
     )(
         block_index,
-        shifts,
         shifts.reshape(1, count),
         starts.reshape(1, nsize),
         tensor_blocks.reshape(slots, side, side),
     )
+    iterate, estimate = pl.pallas_call(
+        tail,
+        out_shape=(
+            jax.ShapeDtypeStruct((1, nsize), f32),
+            jax.ShapeDtypeStruct((1, 1), f32),
+        ),
+        name="tail",
+    )(rows)
     return iterate.reshape(nsize, 1), estimate.reshape(1)
 
 

time: 61.9 us -> 57.5 us (0.929)
  between operations: 2.4 us -> 0.64 us
  Pallas kernels: 58.1 us -> 56.7 us
  local copies, waits for them, and re-layouts: 1.22 us -> 0 us
    pallas_call x1, Pallas kernels: 58.1 us -> 55.5 us  [body(): pl.pallas_call(functools.partial(kernel, (slots, bs, nsize, count), torus...]
    pallas_call x0 -> x1, Pallas kernels: none -> 1.26 us  [body(): pl.pallas_call(tail, out_shape=(jax.ShapeDtypeStruct((1, nsize), f32), ja...]
    unnamed x1 -> x0, local copies, waits for them, and re-layouts: 1.22 us -> none
where the time goes in v2:
time: 57.5 us; the launch traced here: 57.4 us
  Pallas kernels  56.7 us (99%)
  between operations  0.64 us (1%)
    pallas_call x1, Pallas kernels, body(): pl.pallas_call(functools.partial(kernel, (slots, bs, nsize, count), torus...  55.5 us
    pallas_call x1, Pallas kernels, body(): pl.pallas_call(tail, out_shape=(jax.ShapeDtypeStruct((1, nsize), f32), ja...  1.26 us

profile of v2, /device:TPU:1, one launch (start us, length us, event | category | flops | bytes accessed | tf_op | source)
XLA Modules:
  0.0 57.4 jit_solution(5552288799069133195)
XLA Ops:
  0.6 55.5 %power.1.rows_ref = f32[2,256]{1,0:T(2,128)} custom-call(s32[2,4]{1,0:T(2,128)} %bi_hbm.1, f32[1,256]{1,0:T(1,128)} %bitcast.6, f32[1,256]{1,0:T(1,128)} %bitcast.7, bf16[2,1024,1024]{2,1,0:T(8,128)(2,1)} %bitcast.5), custom_call_target="tpu_custom_call" | custom-call | tf_op jit(solution)/shard_map/power/pallas_call | solution.py:278
  56.1 1.3 %tail.1 = (f32[1,256]{1,0:T(1,128)}, f32[1,1]{1,0:T(1,128)}) custom-call(f32[2,256]{1,0:T(2,128)} %power.1.rows_ref), custom_call_target="tpu_custom_call" | custom-call | tf_op jit(solution)/shard_map/tail/pallas_call | solution.py:323

commit v3 on v2

--- a/solution.py
+++ b/solution.py
@@ -85,17 +85,19 @@
         load.start()
         loads.append(load)
 
+    def hops(step, size):
+        return min(step, size - step)
+
+    steps = [(dy, dx, dc) for dy in range(ny) for dx in range(nx) for dc in range(nc)][1:]
+    steps.sort(key=lambda d: -(hops(d[0], ny) + hops(d[1], nx)))
     plane = []
-    for dy in range(ny):
-        for dx in range(nx):
-            for dc in range(nc):
-                if dy or dx or dc:
-                    py = lax.rem(y + dy, ny)
-                    px = lax.rem(x + dx, nx)
-                    pc = lax.rem(c + dc, nc)
-                    plane.append(((py, z, px, pc), (py * nx + px) * nc + pc))
+    for dy, dx, dc in steps:
+        py = lax.rem(y + dy, ny)
+        px = lax.rem(x + dx, nx)
+        pc = lax.rem(c + dc, nc)
+        plane.append(((py, z, px, pc), (py * nx + px) * nc + pc))
     line = []
-    for dz in range(1, nz):
+    for dz in sorted(range(1, nz), key=lambda d: -hops(d, nz)):
         pz = lax.rem(z + dz, nz)
         line.append(((y, pz, x, c), pz))
 

time: 57.5 us -> 54.5 us (0.948)
  Pallas kernels: 56.7 us -> 53.8 us
    pallas_call x1, Pallas kernels: 55.5 us -> 52.5 us  [body(): pl.pallas_call(functools.partial(kernel, (slots, bs, nsize, count), torus...]
where the time goes in v3:
time: 54.5 us; the launch traced here: 54.4 us
  Pallas kernels  53.8 us (99%)
  between operations  0.64 us (1%)
    pallas_call x1, Pallas kernels, body(): pl.pallas_call(functools.partial(kernel, (slots, bs, nsize, count), torus...  52.5 us
    pallas_call x1, Pallas kernels, body(): pl.pallas_call(tail, out_shape=(jax.ShapeDtypeStruct((1, nsize), f32), ja...  1.26 us

profile of v3, /device:TPU:1, one launch (start us, length us, event | category | flops | bytes accessed | tf_op | source)
XLA Modules:
  0.0 54.4 jit_solution(14336224980268135546)
XLA Ops:
  0.6 52.5 %power.1.rows_ref = f32[2,256]{1,0:T(2,128)} custom-call(s32[2,4]{1,0:T(2,128)} %bi_hbm.1, f32[1,256]{1,0:T(1,128)} %bitcast.6, f32[1,256]{1,0:T(1,128)} %bitcast.7, bf16[2,1024,1024]{2,1,0:T(8,128)(2,1)} %bitcast.5), custom_call_target="tpu_custom_call" | custom-call | tf_op jit(solution)/shard_map/power/pallas_call | solution.py:280
  53.2 1.3 %tail.1 = (f32[1,256]{1,0:T(1,128)}, f32[1,1]{1,0:T(1,128)}) custom-call(f32[2,256]{1,0:T(2,128)} %power.1.rows_ref), custom_call_target="tpu_custom_call" | custom-call | tf_op jit(solution)/shard_map/tail/pallas_call | solution.py:325

commit v4 on v2

--- a/solution.py
+++ b/solution.py
@@ -12,6 +12,16 @@
 TORUS = (4, 8, 4, 2)
 MESH = pl.DeviceIdType.MESH
 EPS = 1e-06
+NEAR = 2
+
+
+def chip_steps(ny, nx):
+    def hops(step):
+        return sum(min(s, n - s) for s, n in zip(step, (ny, nx)))
+
+    steps = [(dy, dx) for dy in range(ny) for dx in range(nx)][1:]
+    steps.sort(key=lambda step: -hops(step))
+    return [d for d in steps if hops(d) > NEAR], [d for d in steps if hops(d) <= NEAR]
 
 
 def normalized(values):
@@ -48,12 +58,16 @@
     zrows,
     ztile,
     cols,
+    handed,
+    merged,
     arrived,
     zsums,
     zpart,
     zparts,
     image,
     flipped,
+    handed2,
+    merged2,
     arrived2,
     zsend,
     zlast,
@@ -71,6 +85,28 @@
     y, z, x, c = (lax.axis_index(name) for name in BLK)
     me = (y * nx + x) * nc + c
 
+    def at(dy, dx, core):
+        py = lax.rem(y + dy, ny)
+        px = lax.rem(x + dx, nx)
+        return (py, z, px, core), (py * nx + px) * nc + core
+
+    far_steps, near_steps = chip_steps(ny, nx)
+    other = 1 - c
+    partner, partner_at = at(0, 0, other)
+    far = [at(dy, dx, core) for dy, dx in far_steps for core in (c, other)]
+    near = [at(dy, dx, c) for dy, dx in near_steps]
+    near_other = [at(dy, dx, other) for dy, dx in near_steps]
+    plane = far + [peer for pair in zip(near, near_other) for peer in pair]
+    plane.append((partner, partner_at))
+    line = []
+    for dz in sorted(range(1, nz), key=lambda d: -min(d, nz - d)):
+        pz = lax.rem(z + dz, nz)
+        line.append(((y, pz, x, c), pz))
+    everyone = [peer for peer, _ in line + plane]
+
+    barrier = pltpu.get_barrier_semaphore()
+    for peer in everyone:
+        pl.semaphore_signal(barrier, inc=1, device_id=peer, device_id_type=MESH)
     own = pltpu.make_async_copy(starts_ref, zrows.at[z], load_sem.at[slots])
     own.start()
     small = [
@@ -85,25 +121,8 @@
         load.start()
         loads.append(load)
 
-    plane = []
-    for dy in range(ny):
-        for dx in range(nx):
-            for dc in range(nc):
-                if dy or dx or dc:
-                    py = lax.rem(y + dy, ny)
-                    px = lax.rem(x + dx, nx)
-                    pc = lax.rem(c + dc, nc)
-                    plane.append(((py, z, px, pc), (py * nx + px) * nc + pc))
-    line = []
-    for dz in range(1, nz):
-        pz = lax.rem(z + dz, nz)
-        line.append(((y, pz, x, c), pz))
-
-    barrier = pltpu.get_barrier_semaphore()
-    for peer, _ in plane + line:
-        pl.semaphore_signal(barrier, inc=1, device_id=peer, device_id_type=MESH)
     own.wait()
-    pl.semaphore_wait(barrier, len(plane) + len(line))
+    pl.semaphore_wait(barrier, len(everyone))
 
     def send(phase, src, dst, peer):
         pltpu.make_async_remote_copy(
@@ -118,6 +137,31 @@
     def wait(sem, span):
         pltpu.make_async_copy(span, span, sem).wait()
 
+    def spread(phase, source, held):
+        for peer, _ in plane:
+            send(phase, source, held.at[me], peer)
+
+    def spread_done(phase, source, held):
+        held[me] = source[...]
+        wait(recv_sem.at[phase], held.at[pl.ds(0, group - 1)])
+
+    def collect(phase, source, handed, merged, got):
+        rows = got.shape[1]
+
+        def piece_of(place):
+            return pl.ds(pl.multiple_of(place * rows, rows), rows)
+
+        for i, (peer, place) in enumerate(far):
+            send(phase + 1, source.at[piece_of(place)], got.at[len(near) + i], peer)
+        for i, (_, place) in enumerate(near_other):
+            send(phase, source.at[piece_of(place)], handed.at[i], partner)
+        send(phase, source.at[piece_of(partner_at)], handed.at[len(near)], partner)
+        wait(recv_sem.at[phase], handed)
+        for i, (peer, place) in enumerate(near):
+            merged[i] = source[piece_of(place), :] + handed[i]
+            send(phase + 1, merged.at[i], got.at[i], peer)
+        return source[piece_of(me), :] + handed[len(near)]
+
     for peer, _ in line:
         send(0, zrows.at[z], zrows.at[z], peer)
 
@@ -132,8 +176,7 @@
 
     wait(recv_sem.at[0], zrows.at[pl.ds(0, nz - 1)])
     ztile[...] = zrows[...].reshape(nz, nsize)
-    for peer, _ in plane:
-        send(1, ztile, cols.at[me], peer)
+    spread(1, ztile, cols)
     for load in small:
         load.wait()
     column = ((y * nz + z) * nx + x) * nc + c
@@ -156,8 +199,7 @@
 
     for s in range(slots):
         flip(s)
-    wait(recv_sem.at[1], cols.at[pl.ds(0, group - 1)])
-    cols[me] = ztile[...]
+    spread_done(1, ztile, cols)
     cur[0] = normalized(cols[...].reshape(starts, nsize).T)
 
     def index(s, position):
@@ -218,45 +260,44 @@
     sums = contract(0)
     for p in range(blocks_count):
         total[p * bs : (p + 1) * bs, :] = sums[p]
-    for peer, other in plane:
-        send(2, total.at[pl.ds(pl.multiple_of(other * piece, piece), piece)], arrived.at[me], peer)
-    arrived[me] = total[pl.ds(pl.multiple_of(me * piece, piece), piece), :]
-    wait(recv_sem.at[2], arrived.at[pl.ds(0, group - 1)])
-    zpart[...] = jnp.sum(arrived[...], axis=0)
+    own_piece = collect(4, total, handed, merged, arrived)
+    wait(recv_sem.at[5], arrived)
+    zpart[...] = own_piece + jnp.sum(arrived[...], axis=0)
     for peer, _ in line:
-        send(3, zpart, zparts.at[z], peer)
+        send(6, zpart, zparts.at[z], peer)
     zparts[z] = zpart[...]
-    wait(recv_sem.at[3], zparts.at[pl.ds(0, nz - 1)])
+    wait(recv_sem.at[6], zparts.at[pl.ds(0, nz - 1)])
     zsums[...] = jnp.sum(zparts[...], axis=0)
-    for peer, _ in plane:
-        send(4, zsums, image.at[me], peer)
-    image[me] = zsums[...]
-    wait(recv_sem.at[4], image.at[pl.ds(0, group - 1)])
+    spread(7, zsums, image)
+    spread_done(7, zsums, image)
     cur[1] = normalized(image[...].reshape(nsize, starts) + shifts * cur[0])
 
     sums = contract(1)
     for p in range(blocks_count):
         flipped[:, p * bs : (p + 1) * bs] = sums[p].T
-    for peer, other in plane:
-        send(5, flipped.at[pl.ds(pl.multiple_of(other * nz, nz), nz)], arrived2.at[me], peer)
-    arrived2[me] = flipped[pl.ds(pl.multiple_of(me * nz, nz), nz), :]
+    own_piece = collect(10, flipped, handed2, merged2, arrived2)
     cols[...] = cur[1].T.reshape(group, nz, nsize)
-    wait(recv_sem.at[5], arrived2.at[pl.ds(0, group - 1)])
-    zsend[...] = jnp.sum(arrived2[...], axis=0).reshape(nz, 1, nsize)
-    for peer, other in line:
-        send(6, zsend.at[other], zlast.at[z], peer)
+    wait(recv_sem.at[11], arrived2)
+    zsend[...] = (own_piece + jnp.sum(arrived2[...], axis=0)).reshape(nz, 1, nsize)
+    for peer, place in line:
+        send(12, zsend.at[place], zlast.at[z], peer)
     zlast[z] = zsend[z]
     previous = cols[me, pl.ds(z, 1), :]
-    wait(recv_sem.at[6], zlast.at[pl.ds(0, nz - 1)])
+    wait(recv_sem.at[12], zlast.at[pl.ds(0, nz - 1)])
     mine = jnp.sum(zlast[...], axis=0)
     last = mine + own_shift * previous
     out_ref[0:1, :] = last * lax.rsqrt(jnp.mean(last * last, axis=1, keepdims=True) + EPS)
     scale = lax.rsqrt(jnp.mean(mine * mine, axis=1, keepdims=True) + EPS)
     out_ref[1:2, :] = previous * mine * (scale / nsize)
 
-    spans = (zrows, cols, arrived, zparts, image, arrived2, zlast)
-    for phase, span in enumerate(spans):
-        wait(send_sem.at[phase], span.at[pl.ds(0, span.shape[0] - 1)])
+    sent = [(0, zrows, nz - 1), (6, zparts, nz - 1), (12, zlast, nz - 1)]
+    for phase, span in ((1, cols), (7, image)):
+        sent.append((phase, span, group - 1))
+    for phase, span, span2 in ((4, handed, arrived), (10, handed2, arrived2)):
+        sent += [(phase, span, len(near) + 1), (phase + 1, span2, len(near) + len(far))]
+    for phase, span, count in sent:
+        if count:
+            wait(send_sem.at[phase], span.at[pl.ds(0, count)])
 
 
 def tail(rows_ref, out_ref, est_ref):
@@ -274,7 +315,9 @@
     side = bs * bs
     f32 = jnp.float32
     vmem = pltpu.MemorySpace.VMEM
-    phases = 7
+    far, near = (len(part) for part in chip_steps(ny, nx))
+    far = far * nc
+    phases = 13
     (rows,) = pl.pallas_call(
         functools.partial(kernel, (slots, bs, nsize, count), torus),
         out_shape=(
@@ -297,13 +340,17 @@
             pltpu.VMEM((nz, 1, nsize), f32),
             pltpu.VMEM((nz, nsize), f32),
             pltpu.VMEM((group, nz, nsize), f32),
-            pltpu.VMEM((group, piece, count), f32),
+            pltpu.VMEM((near + 1, piece, count), f32),
+            pltpu.VMEM((near, piece, count), f32),
+            pltpu.VMEM((near + far, piece, count), f32),
             pltpu.VMEM((piece, count), f32),
             pltpu.VMEM((piece, count), f32),
             pltpu.VMEM((nz, piece, count), f32),
             pltpu.VMEM((group, piece, count), f32),
             pltpu.VMEM((count, nsize), f32),
-            pltpu.VMEM((group, nz, nsize), f32),
+            pltpu.VMEM((near + 1, nz, nsize), f32),
+            pltpu.VMEM((near, nz, nsize), f32),
+            pltpu.VMEM((near + far, nz, nsize), f32),
             pltpu.VMEM((nz, 1, nsize), f32),
             pltpu.VMEM((nz, 1, nsize), f32),
             pltpu.VMEM(block_index.shape, jnp.int32),

time: 57.5 us -> 54.6 us (0.950)
  Pallas kernels: 56.7 us -> 53.8 us
    pallas_call x1, Pallas kernels: 55.5 us -> 52.6 us  [body(): pl.pallas_call(functools.partial(kernel, (slots, bs, nsize, count), torus...]
where the time goes in v4:
time: 54.6 us; the launch traced here: 54.5 us
  Pallas kernels  53.8 us (99%)
  between operations  0.64 us (1%)
    pallas_call x1, Pallas kernels, body(): pl.pallas_call(functools.partial(kernel, (slots, bs, nsize, count), torus...  52.6 us
    pallas_call x1, Pallas kernels, body(): pl.pallas_call(tail, out_shape=(jax.ShapeDtypeStruct((1, nsize), f32), ja...  1.26 us

profile of v4, /device:TPU:1, one launch (start us, length us, event | category | flops | bytes accessed | tf_op | source)
XLA Modules:
  0.0 54.5 jit_solution(2101124608535170125)
XLA Ops:
  0.6 52.6 %power.1.rows_ref = f32[2,256]{1,0:T(2,128)} custom-call(s32[2,4]{1,0:T(2,128)} %bi_hbm.1, f32[1,256]{1,0:T(1,128)} %bitcast.6, f32[1,256]{1,0:T(1,128)} %bitcast.7, bf16[2,1024,1024]{2,1,0:T(8,128)(2,1)} %bitcast.5), custom_call_target="tpu_custom_call" | custom-call | tf_op jit(solution)/shard_map/power/pallas_call | solution.py:321
  53.2 1.3 %tail.1 = (f32[1,256]{1,0:T(1,128)}, f32[1,1]{1,0:T(1,128)}) custom-call(f32[2,256]{1,0:T(2,128)} %power.1.rows_ref), custom_call_target="tpu_custom_call" | custom-call | tf_op jit(solution)/shard_map/tail/pallas_call | solution.py:370

commit v5 on v4

--- a/solution.py
+++ b/solution.py
@@ -359,7 +359,7 @@
             pltpu.SemaphoreType.DMA((phases,)),
             pltpu.SemaphoreType.DMA((slots + 3,)),
         ],
-        compiler_params=pltpu.CompilerParams(collective_id=0, has_side_effects=True),
+        compiler_params=pltpu.CompilerParams(collective_id=0, has_side_effects=True, vmem_limit_bytes=63963136),
         name="power",
     )(
         block_index,
@@ -373,6 +373,7 @@
             jax.ShapeDtypeStruct((1, nsize), f32),
             jax.ShapeDtypeStruct((1, 1), f32),
         ),
+        compiler_params=pltpu.CompilerParams(vmem_limit_bytes=1024 * 1024),
         name="tail",
     )(rows)
     return iterate.reshape(nsize, 1), estimate.reshape(1)

time: 54.6 us -> 54.5 us (level)
  Pallas kernels: 53.8 us -> 53.1 us
  local copies, waits for them, and re-layouts: 0 us -> 0.65 us
    pallas_call x1, Pallas kernels: 1.26 us -> 0.59 us  [body(): pl.pallas_call(tail, out_shape=(jax.ShapeDtypeStruct((1, nsize), f32), ja...]
    unnamed x0 -> x2, local copies, waits for them, and re-layouts: none -> 0.65 us
where the time goes in v5:
time: 54.5 us; the launch traced here: 54.4 us
  Pallas kernels  53.1 us (97%)
  local copies, waits for them, and re-layouts  0.65 us (1%)
  between operations  0.65 us (1%)
    pallas_call x1, Pallas kernels, body(): pl.pallas_call(functools.partial(kernel, (slots, bs, nsize, count), torus...  52.6 us

profile of v5, /device:TPU:1, one launch (start us, length us, event | category | flops | bytes accessed | tf_op | source)
XLA Modules:
  0.0 54.4 jit_solution(12492950894640249531)
XLA Ops:
  0.6 52.6 %power.1.rows_ref = f32[2,256]{1,0:T(2,128)} custom-call(s32[2,4]{1,0:T(2,128)} %bi_hbm.1, f32[1,256]{1,0:T(1,128)} %bitcast.6, f32[1,256]{1,0:T(1,128)} %bitcast.7, bf16[2,1024,1024]{2,1,0:T(8,128)(2,1)} %bitcast.5), custom_call_target="tpu_custom_call" | custom-call | tf_op jit(solution)/shard_map/power/pallas_call | solution.py:321
  53.2 0.0 copy-start
  53.2 0.6 %copy-done = f32[2,256]{1,0:T(2,128)S(1)} copy-done((f32[2,256]{1,0:T(2,128)S(1)}, f32[2,256]{1,0:T(2,128)}, u32[]{:S(2)}) %copy-start) | copy-done | bytes 2072
  53.8 0.6 %tail.1 = (f32[1,256]{1,0:T(1,128)}, f32[1,1]{1,0:T(1,128)}) custom-call(f32[2,256]{1,0:T(2,128)S(1)} %copy-done), custom_call_target="tpu_custom_call" | custom-call | tf_op jit(solution)/shard_map/tail/pallas_call | solution.py:370
Async XLA Ops:
  53.2 0.7 %copy-start = (f32[2,256]{1,0:T(2,128)S(1)}, f32[2,256]{1,0:T(2,128)}, u32[]{:S(2)}) copy-start(f32[2,256]{1,0:T(2,128)} %power.1.rows_ref) | copy-start | bytes 6148
